TPU v7x, 32 devices: a whole 2x2x4 slice. The times are simulated.
32 devices in a mesh: seq: 8 (over z, x), head: 4 (over y, core).
Axes of the slice: x: 2, y: 2, z: 4, core: 2. Of those that a mesh axis runs over, the one named last changes fastest.
Arguments:
- queries: bfloat16 [1024, 1024], P('seq', 'head'), may hold values from -6 to 6
- keys: bfloat16 [1024, 1024], P('seq', 'head'), may hold values from -6 to 6
- values: bfloat16 [1024, 1024], P('seq', 'head'), may hold values from -3 to 3
- out_grad: bfloat16 [1024, 1024], P('seq', 'head'), may hold values from -3 to 3
- w_query: bfloat16 [1024, 2048], P('head'), may hold values from -0.1875 to 0.1875
- w_key: bfloat16 [1024, 2048], P('head'), may hold values from -0.1875 to 0.1875
- w_value: bfloat16 [1024, 2048], P('head'), may hold values from -0.1875 to 0.1875
Outputs:
- input_grad: bfloat16 [1024, 2048], P('seq', 'head')
All inputs are finite; a program needn't handle non-finite values.
Results may differ from a plain program's by a relative error of at most 0.0064.
Values sent between devices are 32-bit elements; how exact they have to be, the bound alone decides.
A program may use at most 128 MiB of HBM per device.

v0:
```python
import functools

import jax
import jax.numpy as jnp
import numpy as np
from jax import lax
from jax.experimental import pallas as pl
from jax.experimental.pallas import tpu as pltpu
from jax.sharding import PartitionSpec as P

HD = 64
MESH = pl.DeviceIdType.MESH


def shifted(value, axis, steps):
    count = lax.axis_size(axis)
    leading, last = (max(0, -steps), min(count, count - steps))
    return lax.ppermute(value, axis, [(source, source + steps) for source in range(leading, last)])


def pair_tables(width):
    first, second = np.triu_indices(width)
    count = first.shape[0]
    select_first = np.zeros((width, count), np.float32)
    select_second = np.zeros((width, count), np.float32)
    select_first[first, np.arange(count)] = 1.0
    select_second[second, np.arange(count)] = 1.0
    scaling = np.where(first == second, 1.0, np.sqrt(2.0)) / width
    return (select_first, select_second, scaling.astype(np.float32))


def expand_features(inputs, pick_first, pick_second, scaling):
    first = jnp.dot(inputs, pick_first, preferred_element_type=jnp.bfloat16)
    second = jnp.dot(inputs, pick_second, preferred_element_type=jnp.bfloat16)
    feats = (first.astype(jnp.float32) * second.astype(jnp.float32) * scaling).astype(jnp.bfloat16)
    return (first, second, feats)


def chain_back(first, second, dphi, back_first, back_second, scaling):
    scaled = dphi * scaling
    left = scaled * second.astype(jnp.float32)
    right = scaled * first.astype(jnp.float32)
    return jnp.dot(
        left, back_first, precision=lax.Precision.HIGHEST, preferred_element_type=jnp.float32
    ) + jnp.dot(
        right, back_second, precision=lax.Precision.HIGHEST, preferred_element_type=jnp.float32
    )


def on_device(queries, keys, values, out_grad, w_query, w_key, w_value):
    count_rows = queries.shape[0]
    head_count = queries.shape[1] // HD
    select_first, select_second, scale_np = pair_tables(HD)
    pick_first = jnp.asarray(select_first, jnp.bfloat16)
    pick_second = jnp.asarray(select_second, jnp.bfloat16)
    back_first = jnp.asarray(select_first.T, jnp.float32)
    back_second = jnp.asarray(select_second.T, jnp.float32)
    scaling = jnp.asarray(scale_np, jnp.float32)
    feat_count = scale_np.shape[0]
    query_heads = queries.reshape(count_rows, head_count, HD)
    key_heads = keys.reshape(count_rows, head_count, HD)
    value_heads = values.reshape(count_rows, head_count, HD)
    grad_heads = out_grad.reshape(count_rows, head_count, HD)
    query_expanded = []
    key_expanded = []
    kv_parts = []
    grad_parts = []
    for number in range(head_count):
        query_set = expand_features(query_heads[:, number], pick_first, pick_second, scaling)
        key_set = expand_features(key_heads[:, number], pick_first, pick_second, scaling)
        query_expanded.append(query_set)
        key_expanded.append(key_set)
        kv_parts.append(
            jnp.einsum(
                "tf,td->fd", key_set[2], value_heads[:, number], preferred_element_type=jnp.float32
            )
        )
        grad_parts.append(
            jnp.einsum(
                "tf,td->fd", query_set[2], grad_heads[:, number], preferred_element_type=jnp.float32
            )
        )
    kv_local = jnp.stack(kv_parts, 1).reshape(feat_count, head_count * HD)
    grad_local = jnp.stack(grad_parts, 1).reshape(feat_count, head_count * HD)
    rounds = (lax.axis_size("seq") - 1).bit_length()
    kv_running = kv_local
    grad_running = grad_local
    for level in range(rounds):
        kv_running = kv_running + shifted(kv_running, "seq", 1 << level)
        grad_running = grad_running + shifted(grad_running, "seq", -(1 << level))
    kv_before = kv_running - kv_local
    grad_after = grad_running - grad_local
    kv_before = kv_before.astype(jnp.bfloat16).reshape(feat_count, head_count, HD)
    grad_after = grad_after.astype(jnp.bfloat16).reshape(feat_count, head_count, HD)
    causal = lax.broadcasted_iota(jnp.int32, (count_rows, count_rows), 0) >= lax.broadcasted_iota(
        jnp.int32, (count_rows, count_rows), 1
    )
    scores = jnp.einsum("thd,shd->hts", query_heads, key_heads, preferred_element_type=jnp.float32)
    products = jnp.einsum(
        "thd,shd->hts", grad_heads, value_heads, preferred_element_type=jnp.float32
    )
    attn = jnp.where(causal, (scores / HD) ** 2, 0.0).astype(jnp.bfloat16)
    pgrad = jnp.where(causal, 2.0 * scores * products / (HD * HD), 0.0).astype(jnp.bfloat16)
    query_local = jnp.einsum("hts,shd->thd", pgrad, key_heads, preferred_element_type=jnp.float32)
    key_local = jnp.einsum("hts,thd->shd", pgrad, query_heads, preferred_element_type=jnp.float32)
    value_local = jnp.einsum("hts,thd->shd", attn, grad_heads, preferred_element_type=jnp.float32)
    query_out = []
    key_out = []
    value_out = []
    for number in range(head_count):
        qfirst, qsecond, query_feat = query_expanded[number]
        kfirst, ksecond, key_feat = key_expanded[number]
        dfq = jnp.einsum(
            "td,fd->tf",
            grad_heads[:, number],
            kv_before[:, number],
            preferred_element_type=jnp.float32,
        )
        dfk = jnp.einsum(
            "td,fd->tf",
            value_heads[:, number],
            grad_after[:, number],
            preferred_element_type=jnp.float32,
        )
        query_out.append(
            query_local[:, number]
            + chain_back(qfirst, qsecond, dfq, back_first, back_second, scaling)
        )
        key_out.append(
            key_local[:, number]
            + chain_back(kfirst, ksecond, dfk, back_first, back_second, scaling)
        )
        value_out.append(
            value_local[:, number]
            + jnp.einsum(
                "tf,fd->td", key_feat, grad_after[:, number], preferred_element_type=jnp.float32
            )
        )
    query_grad = jnp.stack(query_out, 1).astype(jnp.bfloat16).reshape(count_rows, head_count * HD)
    key_grad = jnp.stack(key_out, 1).astype(jnp.bfloat16).reshape(count_rows, head_count * HD)
    value_grad = jnp.stack(value_out, 1).astype(jnp.bfloat16).reshape(count_rows, head_count * HD)
    partial_sum = jnp.dot(query_grad, w_query, preferred_element_type=jnp.float32)
    partial_sum = partial_sum + jnp.dot(key_grad, w_key, preferred_element_type=jnp.float32)
    partial_sum = partial_sum + jnp.dot(value_grad, w_value, preferred_element_type=jnp.float32)
    return lax.psum_scatter(partial_sum, "head", scatter_dimension=1, tiled=True).astype(
        jnp.bfloat16
    )


def stacked(block):
    lanes = lax.broadcasted_iota(jnp.int32, block.shape, 1)
    low = jnp.where(lanes < HD, block, 0.0).astype(jnp.bfloat16)
    high = jnp.where(lanes >= HD, block, 0.0).astype(jnp.bfloat16)
    return jnp.concatenate([low, high], axis=0)


def rows_dot(left, right):
    return lax.dot_general(
        left, right, (((1,), (1,)), ((), ())), preferred_element_type=jnp.float32
    )


def direct_kernel(
    n_seq,
    queries,
    keys,
    values,
    grads,
    wq_hbm,
    wk_hbm,
    wv_hbm,
    out,
    buffers,
    weights,
    totals,
    own_part,
    core_send,
    core_recv,
    far_send,
    far_recv,
    recv_sem,
    line_sem,
    side_sem,
    weight_sem,
    reduce_send_sem,
    reduce_recv_sem,
):
    K, V, Q, G = range(4)
    rows, width = queries.shape
    lines = n_seq // 2
    me = lax.axis_index("seq")
    line, side = me // 2, me % 2
    other = 2 * line + (1 - side)
    head = lax.axis_index("head")
    far, core = head // 2, head % 2
    core_mate = 2 * far + (1 - core)
    far_mate = 2 * (1 - far) + core
    out_width = out.shape[1]

    weight_copies = [
        pltpu.make_async_copy(source, weights.at[i], weight_sem.at[i])
        for i, source in enumerate((wq_hbm, wk_hbm, wv_hbm))
    ]
    for copy in weight_copies:
        copy.start()

    for which, ref in ((K, keys), (V, values), (Q, queries), (G, grads)):
        buffers[which, me] = ref[...].astype(jnp.float32)

    barrier = pltpu.get_barrier_semaphore()

    def greet(target):
        pl.semaphore_signal(barrier, inc=1, device_id=target, device_id_type=MESH)

    greet({"seq": other})
    greet({"head": core_mate})
    greet({"head": far_mate})
    has_up = line < lines - 1
    has_down = line > 0

    @pl.when(has_up)
    def _():
        greet({"seq": me + 2})

    @pl.when(has_down)
    def _():
        greet({"seq": me - 2})

    pl.semaphore_wait(barrier, 3 + has_up.astype(jnp.int32) + has_down.astype(jnp.int32))

    def transfer(which, block, sem, target):
        return pltpu.make_async_remote_copy(
            src_ref=buffers.at[which, block],
            dst_ref=buffers.at[which, block],
            send_sem=sem.at[which, block],
            recv_sem=recv_sem.at[which, block],
            device_id={"seq": target},
            device_id_type=MESH,
        )

    def along(which, block):
        return transfer(which, block, line_sem, me + 2 if which in (K, V) else me - 2)

    def across(which, block):
        return transfer(which, block, side_sem, other)

    def each_send(step, act):
        for pair in ((K, Q), (V, G)):
            for which in pair:
                rising = which in (K, V)
                block = me - 2 * step if rising else me + 2 * step
                present = (line >= step) if rising else (line + step < lines)
                onward = has_up if rising else has_down

                def body(which=which, block=block, rising=rising, onward=onward):
                    if step and act == "start":
                        along(which, block).wait_recv()

                    @pl.when(onward)
                    def _():
                        copy = along(which, block)
                        copy.start() if act == "start" else copy.wait_send()

                    def cross():
                        copy = across(which, block)
                        copy.start() if act == "start" else copy.wait_send()

                    if step:
                        cross()
                    else:
                        pl.when(side == (0 if rising else 1))(cross)

                if step:
                    pl.when(present)(body)
                else:
                    body()

    def query_role(block, diagonal=False):
        for cols in range(0, width, 2 * HD):
            part = slice(cols, cols + 2 * HD)
            k2 = stacked(buffers[K, block, :, part])
            v2 = stacked(buffers[V, block, :, part])
            scores = rows_dot(queries[:, part], k2)
            products = rows_dot(grads[:, part], v2)
            weight = scores * products * (2.0 / (HD * HD))
            if diagonal:
                t = lax.broadcasted_iota(jnp.int32, weight.shape, 0)
                s = lax.broadcasted_iota(jnp.int32, weight.shape, 1) % rows
                weight = jnp.where(t >= s, weight, 0.0)
            result = jnp.dot(
                weight.astype(jnp.bfloat16), k2, preferred_element_type=jnp.float32
            )
            if diagonal:
                totals[0, :, part] = result
            else:
                totals[0, :, part] += result

    def key_role(block, diagonal=False):
        for cols in range(0, width, 2 * HD):
            part = slice(cols, cols + 2 * HD)
            q2 = stacked(buffers[Q, block, :, part])
            g2 = stacked(buffers[G, block, :, part])
            scores = rows_dot(keys[:, part], q2)
            products = rows_dot(values[:, part], g2)
            weight = scores * products * (2.0 / (HD * HD))
            attn = (scores * (1.0 / HD)) * (scores * (1.0 / HD))
            if diagonal:
                s = lax.broadcasted_iota(jnp.int32, weight.shape, 0)
                t = lax.broadcasted_iota(jnp.int32, weight.shape, 1) % rows
                weight = jnp.where(t >= s, weight, 0.0)
                attn = jnp.where(t >= s, attn, 0.0)
            key_result = jnp.dot(
                weight.astype(jnp.bfloat16), q2, preferred_element_type=jnp.float32
            )
            value_result = jnp.dot(
                attn.astype(jnp.bfloat16), g2, preferred_element_type=jnp.float32
            )
            if diagonal:
                totals[1, :, part] = key_result
                totals[2, :, part] = value_result
            else:
                totals[1, :, part] += key_result
                totals[2, :, part] += value_result

    def crossed(step):
        kv_block = other - 2 * step
        qg_block = other + 2 * step

        def take_kv():
            across(K, kv_block).wait_recv()
            across(V, kv_block).wait_recv()
            query_role(kv_block)

        def take_qg():
            across(Q, qg_block).wait_recv()
            across(G, qg_block).wait_recv()
            key_role(qg_block)

        if step:
            pl.when(line >= step)(take_kv)
            pl.when(line + step < lines)(take_qg)
        else:
            pl.when(side == 1)(take_kv)
            pl.when(side == 0)(take_qg)

    each_send(0, "start")
    query_role(me, diagonal=True)
    key_role(me, diagonal=True)
    for step in range(1, lines):
        each_send(step, "start")

        @pl.when(line >= step)
        def _():
            query_role(me - 2 * step)

        @pl.when(line + step < lines)
        def _():
            key_role(me + 2 * step)

        crossed(step - 1)
    crossed(lines - 1)

    for copy in weight_copies:
        copy.wait()
    final = [totals[i].astype(jnp.bfloat16) for i in range(3)]

    def project(target):
        cols = pl.ds(pl.multiple_of(target * out_width, out_width), out_width)
        return sum(
            jnp.dot(final[i], weights[i, :, cols], preferred_element_type=jnp.float32)
            for i in range(3)
        )

    def to_core(slot):
        return pltpu.make_async_remote_copy(
            src_ref=core_send.at[slot],
            dst_ref=core_recv.at[slot],
            send_sem=reduce_send_sem.at[slot],
            recv_sem=reduce_recv_sem.at[slot],
            device_id={"head": core_mate},
            device_id_type=MESH,
        )

    to_far = pltpu.make_async_remote_copy(
        src_ref=far_send,
        dst_ref=far_recv,
        send_sem=reduce_send_sem.at[2],
        recv_sem=reduce_recv_sem.at[2],
        device_id={"head": far_mate},
        device_id_type=MESH,
    )
    core_send[0] = project(2 * (1 - far) + (1 - core))
    to_core(0).start()
    far_send[...] = project(far_mate)
    core_send[1] = project(core_mate)
    to_core(0).wait_recv()
    far_send[...] += core_recv[0]
    to_far.start()
    to_core(1).start()
    own_part[...] = project(head)
    to_core(1).wait_recv()
    own_part[...] += core_recv[1]
    to_far.wait_recv()
    out[...] = (own_part[...] + far_recv[...]).astype(out.dtype)

    to_core(0).wait_send()
    to_core(1).wait_send()
    to_far.wait_send()
    for step in range(lines):
        each_send(step, "finish")


def direct_form(n_seq, n_head, queries, keys, values, out_grad, w_query, w_key, w_value):
    rows, width = queries.shape
    model = w_query.shape[1]
    out_width = model // n_head
    vmem = pl.BlockSpec(memory_space=pltpu.VMEM)
    hbm = pl.BlockSpec(memory_space=pl.ANY)
    piece = (rows, out_width)
    return pl.pallas_call(
        functools.partial(direct_kernel, n_seq),
        out_shape=jax.ShapeDtypeStruct(piece, jnp.bfloat16),
        in_specs=[vmem] * 4 + [hbm] * 3,
        out_specs=vmem,
        scratch_shapes=[
            pltpu.VMEM((4, n_seq, rows, width), jnp.float32),
            pltpu.VMEM((3, width, model), jnp.bfloat16),
            pltpu.VMEM((3, rows, width), jnp.float32),
            pltpu.VMEM(piece, jnp.float32),
            pltpu.VMEM((2,) + piece, jnp.float32),
            pltpu.VMEM((2,) + piece, jnp.float32),
            pltpu.VMEM(piece, jnp.float32),
            pltpu.VMEM(piece, jnp.float32),
            pltpu.SemaphoreType.DMA((4, n_seq)),
            pltpu.SemaphoreType.DMA((4, n_seq)),
            pltpu.SemaphoreType.DMA((4, n_seq)),
            pltpu.SemaphoreType.DMA((3,)),
            pltpu.SemaphoreType.DMA((3,)),
            pltpu.SemaphoreType.DMA((3,)),
        ],
        compiler_params=pltpu.CompilerParams(collective_id=0, has_side_effects=True),
    )(queries, keys, values, out_grad, w_query, w_key, w_value)


def solution(mesh):
    placed = (
        P("seq", "head"),
        P("seq", "head"),
        P("seq", "head"),
        P("seq", "head"),
        P("head", None),
        P("head", None),
        P("head", None),
    )
    n_seq, n_head = mesh.shape["seq"], mesh.shape["head"]

    def per_device(queries, *rest):
        rows = queries.shape[0]
        rounds = (n_seq - 1).bit_length()
        direct = (n_seq - 1) * rows < rounds * (HD * (HD + 1) // 2)
        if direct and n_seq % 2 == 0 and n_head == 4:
            return direct_form(n_seq, n_head, queries, *rest)
        return on_device(queries, *rest)

    return jax.shard_map(
        per_device, mesh=mesh, in_specs=placed, out_specs=P("seq", "head"), check_vma=False
    )
```

profile of v0, /device:TPU:0, one launch (start us, length us, event | category | flops | bytes accessed | tf_op | source)
XLA Modules:
  0.0 41.1 jit_solution(7841388082118900521)
XLA Ops:
  0.0 39.5 %shard_map.73 = bf16[128,512]{1,0:T(8,128)(2,1)} custom-call(bf16[128,256]{1,0:T(8,128)(2,1)} %queries.1, bf16[128,256]{1,0:T(8,128)(2,1)} %keys.1, bf16[128,256]{1,0:T(8,128)(2,1)} %values.1, bf16[128,256]{1,0:T(8,128)(2,1)} %grads.1, bf16[256,2048]{1,0:T(8,128)(2,1)} %wq_hbm.1, bf16[256,2048]{1,0:T(8,128)(2,1)} %wk_hbm.1, bf16[256,2048]{1,0:T(8,128)(2,1)} %wv_hbm.1), custom_call_target="tpu_custom_call" | custom-call | tf_op jit(solution)/shard_map/pallas_call | solution.py:420
  39.5 1.6 %copy.9 = bf16[128,512]{1,0:T(8,128)(2,1)} copy(bf16[128,512]{1,0:T(8,128)(2,1)} %shard_map.73) | data formatting | bytes 262144
where the time goes:
time: 41.3 us; the launch traced here: 41.1 us
  Pallas kernels  39.5 us (96%)
  local copies, waits for them, and re-layouts  1.57 us (4%)
    pallas_call x1, Pallas kernels, direct_form(): pl.pallas_call(functools.partial(direct_kernel, n_seq), out_shape=jax.Sha...  39.5 us
    unnamed x1, local copies, waits for them, and re-layouts  1.57 us

commit v1 on v0

--- a/solution.py
+++ b/solution.py
@@ -162,14 +162,15 @@
 
 def direct_kernel(
     n_seq,
-    queries,
-    keys,
-    values,
-    grads,
+    q_hbm,
+    k_hbm,
+    v_hbm,
+    g_hbm,
     wq_hbm,
     wk_hbm,
     wv_hbm,
     out,
+    own,
     buffers,
     weights,
     totals,
@@ -181,12 +182,14 @@
     recv_sem,
     line_sem,
     side_sem,
+    own_sem,
     weight_sem,
     reduce_send_sem,
     reduce_recv_sem,
 ):
     K, V, Q, G = range(4)
-    rows, width = queries.shape
+    unused, rows, width = own.shape
+    pairs = width // (2 * HD)
     lines = n_seq // 2
     me = lax.axis_index("seq")
     line, side = me // 2, me % 2
@@ -196,6 +199,33 @@
     core_mate = 2 * far + (1 - core)
     far_mate = 2 * (1 - far) + core
     out_width = out.shape[1]
+    has_up = line < lines - 1
+    has_down = line > 0
+    lower, upper = 2 * line < lines, 2 * line >= lines
+
+    own_copies = [
+        pltpu.make_async_copy(source, own.at[i], own_sem.at[i])
+        for i, source in enumerate((k_hbm, v_hbm, q_hbm, g_hbm))
+    ]
+    for copy in own_copies:
+        copy.start()
+
+    barrier = pltpu.get_barrier_semaphore()
+
+    def greet(target):
+        pl.semaphore_signal(barrier, inc=1, device_id=target, device_id_type=MESH)
+
+    greet({"seq": other})
+    greet({"head": core_mate})
+    greet({"head": far_mate})
+
+    @pl.when(has_up)
+    def _():
+        greet({"seq": me + 2})
+
+    @pl.when(has_down)
+    def _():
+        greet({"seq": me - 2})
 
     weight_copies = [
         pltpu.make_async_copy(source, weights.at[i], weight_sem.at[i])
@@ -203,85 +233,116 @@
     ]
     for copy in weight_copies:
         copy.start()
-
-    for which, ref in ((K, keys), (V, values), (Q, queries), (G, grads)):
-        buffers[which, me] = ref[...].astype(jnp.float32)
-
-    barrier = pltpu.get_barrier_semaphore()
-
-    def greet(target):
-        pl.semaphore_signal(barrier, inc=1, device_id=target, device_id_type=MESH)
-
-    greet({"seq": other})
-    greet({"head": core_mate})
-    greet({"head": far_mate})
-    has_up = line < lines - 1
-    has_down = line > 0
-
-    @pl.when(has_up)
-    def _():
-        greet({"seq": me + 2})
-
-    @pl.when(has_down)
-    def _():
-        greet({"seq": me - 2})
+    for which, copy in enumerate(own_copies):
+        copy.wait()
+        for p in range(pairs):
+            buffers[which, me, p] = own[which, :, 2 * HD * p : 2 * HD * (p + 1)].astype(
+                jnp.float32
+            )
 
     pl.semaphore_wait(barrier, 3 + has_up.astype(jnp.int32) + has_down.astype(jnp.int32))
 
-    def transfer(which, block, sem, target):
+    def transfer(which, block, p, sem, target):
         return pltpu.make_async_remote_copy(
-            src_ref=buffers.at[which, block],
-            dst_ref=buffers.at[which, block],
-            send_sem=sem.at[which, block],
-            recv_sem=recv_sem.at[which, block],
+            src_ref=buffers.at[which, block, p],
+            dst_ref=buffers.at[which, block, p],
+            send_sem=sem.at[which, block, p],
+            recv_sem=recv_sem.at[which, block, p],
             device_id={"seq": target},
             device_id_type=MESH,
         )
 
-    def along(which, block):
-        return transfer(which, block, line_sem, me + 2 if which in (K, V) else me - 2)
-
-    def across(which, block):
-        return transfer(which, block, side_sem, other)
-
-    def each_send(step, act):
-        for pair in ((K, Q), (V, G)):
-            for which in pair:
-                rising = which in (K, V)
-                block = me - 2 * step if rising else me + 2 * step
-                present = (line >= step) if rising else (line + step < lines)
-                onward = has_up if rising else has_down
-
-                def body(which=which, block=block, rising=rising, onward=onward):
-                    if step and act == "start":
-                        along(which, block).wait_recv()
-
-                    @pl.when(onward)
-                    def _():
-                        copy = along(which, block)
-                        copy.start() if act == "start" else copy.wait_send()
-
-                    def cross():
-                        copy = across(which, block)
-                        copy.start() if act == "start" else copy.wait_send()
-
-                    if step:
-                        cross()
-                    else:
-                        pl.when(side == (0 if rising else 1))(cross)
-
-                if step:
-                    pl.when(present)(body)
-                else:
-                    body()
+    def along(which, block, p):
+        return transfer(which, block, p, line_sem, me + 2 if which in (K, V) else me - 2)
+
+    def across(which, block, p):
+        return transfer(which, block, p, side_sem, other)
+
+    def guarded(condition, body):
+        if condition is True:
+            body()
+        elif condition is not False:
+            pl.when(condition)(body)
+
+    def act_on(copy, act):
+        copy.start() if act == "start" else copy.wait_send()
+
+    def visit(step, which, p, act, line_part, side_part):
+        rising = which in (K, V)
+        block = me - 2 * step if rising else me + 2 * step
+        present = (line >= step) if rising else (line + step < lines)
+        onward = has_up if rising else has_down
+        if step == 0:
+            crosses = side == (0 if rising else 1)
+        elif step == 1 or which in (K, Q):
+            crosses = True
+        else:
+            crosses = False if step == lines - 1 else jnp.logical_not(onward)
+
+        def body():
+            if line_part:
+                if step and act == "start":
+                    along(which, block, p).wait_recv()
+                guarded(onward, lambda: act_on(along(which, block, p), act))
+            if side_part:
+                guarded(crosses, lambda: act_on(across(which, block, p), act))
+
+        guarded(present if step else True, body)
+
+    def own_column(step, act):
+        def urgent(first, second):
+            for now, later in zip(first, second):
+                for p in range(pairs):
+                    visit(step, now, p, act, True, True)
+                    visit(step, later, p, act, True, False)
+            for later in second:
+                for p in range(pairs):
+                    visit(step, later, p, act, False, True)
+
+        if step == 1 and act == "start":
+            pl.when(lower & has_down)(lambda: urgent((K, V), (Q, G)))
+            pl.when(upper & has_up)(lambda: urgent((Q, G), (K, V)))
+
+            @pl.when(jnp.logical_not(has_up & has_down))
+            def _():
+                for pair in ((K, Q), (V, G)):
+                    for p in range(pairs):
+                        for which in pair:
+                            visit(step, which, p, act, True, True)
+        else:
+            for pair in ((K, Q), (V, G)):
+                for p in range(pairs):
+                    for which in pair:
+                        visit(step, which, p, act, True, True)
+
+    def other_column(step, act, which):
+        rising = which in (K, V)
+        block = other - 2 * step if rising else other + 2 * step
+        if step == 0:
+            present = side == (1 if rising else 0)
+        else:
+            present = (line >= step) if rising else (line + step < lines)
+        onward = False
+        if 1 <= step < lines - 1 and which in (V, G):
+            onward = has_up if rising else has_down
+            if step < lines - 2:
+                onward = (line < lines - 2) if rising else (line > 1)
+
+        def body():
+            for p in range(pairs):
+                if act == "start":
+                    across(which, block, p).wait_recv()
+                guarded(onward, lambda: act_on(along(which, block, p), act))
+
+        guarded(present, body)
 
     def query_role(block, diagonal=False):
-        for cols in range(0, width, 2 * HD):
-            part = slice(cols, cols + 2 * HD)
-            k2 = stacked(buffers[K, block, :, part])
-            v2 = stacked(buffers[V, block, :, part])
-            scores = rows_dot(queries[:, part], k2)
-            products = rows_dot(grads[:, part], v2)
+        for p in range(pairs):
+            part = slice(2 * HD * p, 2 * HD * (p + 1))
+            k2 = stacked(buffers[K, block, p])
+            v2 = stacked(buffers[V, block, p])
+            scores = rows_dot(own[Q, :, part], k2)
+            products = rows_dot(own[G, :, part], v2)
             weight = scores * products * (2.0 / (HD * HD))
             if diagonal:
                 t = lax.broadcasted_iota(jnp.int32, weight.shape, 0)
@@ -296,12 +357,12 @@
                 totals[0, :, part] += result
 
     def key_role(block, diagonal=False):
-        for cols in range(0, width, 2 * HD):
-            part = slice(cols, cols + 2 * HD)
-            q2 = stacked(buffers[Q, block, :, part])
-            g2 = stacked(buffers[G, block, :, part])
-            scores = rows_dot(keys[:, part], q2)
-            products = rows_dot(values[:, part], g2)
+        for p in range(pairs):
+            part = slice(2 * HD * p, 2 * HD * (p + 1))
+            q2 = stacked(buffers[Q, block, p])
+            g2 = stacked(buffers[G, block, p])
+            scores = rows_dot(own[K, :, part], q2)
+            products = rows_dot(own[V, :, part], g2)
             weight = scores * products * (2.0 / (HD * HD))
             attn = (scores * (1.0 / HD)) * (scores * (1.0 / HD))
             if diagonal:
@@ -322,50 +383,70 @@
                 totals[1, :, part] += key_result
                 totals[2, :, part] += value_result
 
-    def crossed(step):
-        kv_block = other - 2 * step
-        qg_block = other + 2 * step
-
-        def take_kv():
-            across(K, kv_block).wait_recv()
-            across(V, kv_block).wait_recv()
-            query_role(kv_block)
-
-        def take_qg():
-            across(Q, qg_block).wait_recv()
-            across(G, qg_block).wait_recv()
-            key_role(qg_block)
-
-        if step:
-            pl.when(line >= step)(take_kv)
-            pl.when(line + step < lines)(take_qg)
-        else:
-            pl.when(side == 1)(take_kv)
-            pl.when(side == 0)(take_qg)
-
-    each_send(0, "start")
+    def compute_query(step, origin):
+        present = side == 1 if step == 0 else line >= step
+        pl.when(present)(lambda: query_role(origin - 2 * step))
+
+    def compute_key(step, origin):
+        present = side == 0 if step == 0 else line + step < lines
+        pl.when(present)(lambda: key_role(origin + 2 * step))
+
+    def from_side(step, arrays):
+        for which in arrays:
+            other_column(step, "start", which)
+
+    own_column(0, "start")
     query_role(me, diagonal=True)
     key_role(me, diagonal=True)
     for step in range(1, lines):
-        each_send(step, "start")
-
-        @pl.when(line >= step)
-        def _():
-            query_role(me - 2 * step)
-
-        @pl.when(line + step < lines)
-        def _():
-            key_role(me + 2 * step)
-
-        crossed(step - 1)
-    crossed(lines - 1)
+        own_column(step, "start")
+        if step == 1:
+            from_side(0, (V, G, K, Q))
+        else:
+            if step > 2:
+                from_side(step - 1, (V, G))
+            else:
+                pl.when(lower)(lambda: from_side(1, (V, K)))
+                pl.when(upper)(lambda: from_side(1, (G, Q)))
+        compute_query(step, me)
+        compute_key(step, me)
+        if step == 1:
+            compute_query(0, other)
+            compute_key(0, other)
+        elif step == 2:
+            pl.when(lower)(lambda: compute_query(1, other))
+            pl.when(upper)(lambda: compute_key(1, other))
+        else:
+            if step == 3:
+                pl.when(lower)(lambda: from_side(1, (G, Q)))
+                pl.when(upper)(lambda: from_side(1, (V, K)))
+                pl.when(lower)(lambda: compute_key(1, other))
+                pl.when(upper)(lambda: compute_query(1, other))
+            from_side(step - 1, (K, Q))
+            compute_query(step - 1, other)
+            compute_key(step - 1, other)
+    last = lines - 1
+    if last <= 2:
+        if last == 2:
+            pl.when(lower)(lambda: from_side(1, (G, Q)))
+            pl.when(upper)(lambda: from_side(1, (V, K)))
+            pl.when(lower)(lambda: compute_key(1, other))
+            pl.when(upper)(lambda: compute_query(1, other))
+    if last:
+        from_side(last, (K, Q, V, G))
+        compute_query(last, other)
+        compute_key(last, other)
 
     for copy in weight_copies:
         copy.wait()
-    final = [totals[i].astype(jnp.bfloat16) for i in range(3)]
-
-    def project(target):
-        cols = pl.ds(pl.multiple_of(target * out_width, out_width), out_width)
+    final = [totals[i].astype(jnp.bfloat16) for i in (0, 1, 2)]
+
+    chunks = far_send.shape[0]
+    chunk_width = out_width // chunks
+
+    def project(target, first, count):
+        start = target * out_width + first
+        cols = pl.ds(pl.multiple_of(start, chunk_width), count)
         return sum(
             jnp.dot(final[i], weights[i, :, cols], preferred_element_type=jnp.float32)
             for i in range(3)
@@ -381,62 +462,80 @@
             device_id_type=MESH,
         )
 
-    to_far = pltpu.make_async_remote_copy(
-        src_ref=far_send,
-        dst_ref=far_recv,
-        send_sem=reduce_send_sem.at[2],
-        recv_sem=reduce_recv_sem.at[2],
-        device_id={"head": far_mate},
-        device_id_type=MESH,
-    )
-    core_send[0] = project(2 * (1 - far) + (1 - core))
-    to_core(0).start()
-    far_send[...] = project(far_mate)
-    core_send[1] = project(core_mate)
-    to_core(0).wait_recv()
-    far_send[...] += core_recv[0]
-    to_far.start()
-    to_core(1).start()
-    own_part[...] = project(head)
-    to_core(1).wait_recv()
-    own_part[...] += core_recv[1]
-    to_far.wait_recv()
-    out[...] = (own_part[...] + far_recv[...]).astype(out.dtype)
-
-    to_core(0).wait_send()
-    to_core(1).wait_send()
-    to_far.wait_send()
+    def to_far(i):
+        return pltpu.make_async_remote_copy(
+            src_ref=far_send.at[i],
+            dst_ref=far_recv.at[i],
+            send_sem=reduce_send_sem.at[2 * chunks + i],
+            recv_sem=reduce_recv_sem.at[2 * chunks + i],
+            device_id={"head": far_mate},
+            device_id_type=MESH,
+        )
+
+    def pass_far(i):
+        to_core(i).wait_recv()
+        far_send[i] += core_recv[i]
+        to_far(i).start()
+
+    for i in range(chunks):
+        core_send[i] = project(2 * (1 - far) + (1 - core), i * chunk_width, chunk_width)
+        to_core(i).start()
+        far_send[i] = project(far_mate, i * chunk_width, chunk_width)
+        if i:
+            pass_far(i - 1)
+    pass_far(chunks - 1)
+    for i in range(chunks):
+        core_send[chunks + i] = project(core_mate, i * chunk_width, chunk_width)
+        to_core(chunks + i).start()
+    own_part[...] = project(head, 0, out_width)
+    for i in range(chunks):
+        part = slice(i * chunk_width, (i + 1) * chunk_width)
+        to_core(chunks + i).wait_recv()
+        own_part[:, part] += core_recv[chunks + i]
+    for i in range(chunks):
+        part = slice(i * chunk_width, (i + 1) * chunk_width)
+        to_far(i).wait_recv()
+        out[:, part] = (own_part[:, part] + far_recv[i]).astype(out.dtype)
+
+    for i in range(2 * chunks):
+        to_core(i).wait_send()
+    for i in range(chunks):
+        to_far(i).wait_send()
     for step in range(lines):
-        each_send(step, "finish")
+        own_column(step, "finish")
+        for which in (K, V, Q, G):
+            other_column(step, "finish", which)
 
 
 def direct_form(n_seq, n_head, queries, keys, values, out_grad, w_query, w_key, w_value):
     rows, width = queries.shape
     model = w_query.shape[1]
     out_width = model // n_head
-    vmem = pl.BlockSpec(memory_space=pltpu.VMEM)
-    hbm = pl.BlockSpec(memory_space=pl.ANY)
-    piece = (rows, out_width)
+    pairs = width // (2 * HD)
+    chunks = 1
+    piece = (rows, out_width // chunks)
     return pl.pallas_call(
         functools.partial(direct_kernel, n_seq),
-        out_shape=jax.ShapeDtypeStruct(piece, jnp.bfloat16),
-        in_specs=[vmem] * 4 + [hbm] * 3,
-        out_specs=vmem,
+        out_shape=jax.ShapeDtypeStruct((rows, out_width), jnp.bfloat16),
+        in_specs=[pl.BlockSpec(memory_space=pl.ANY)] * 7,
+        out_specs=pl.BlockSpec(memory_space=pltpu.VMEM),
         scratch_shapes=[
-            pltpu.VMEM((4, n_seq, rows, width), jnp.float32),
+            pltpu.VMEM((4, rows, width), jnp.bfloat16),
+            pltpu.VMEM((4, n_seq, pairs, rows, 2 * HD), jnp.float32),
             pltpu.VMEM((3, width, model), jnp.bfloat16),
             pltpu.VMEM((3, rows, width), jnp.float32),
-            pltpu.VMEM(piece, jnp.float32),
-            pltpu.VMEM((2,) + piece, jnp.float32),
-            pltpu.VMEM((2,) + piece, jnp.float32),
-            pltpu.VMEM(piece, jnp.float32),
-            pltpu.VMEM(piece, jnp.float32),
-            pltpu.SemaphoreType.DMA((4, n_seq)),
-            pltpu.SemaphoreType.DMA((4, n_seq)),
-            pltpu.SemaphoreType.DMA((4, n_seq)),
+            pltpu.VMEM((rows, out_width), jnp.float32),
+            pltpu.VMEM((2 * chunks,) + piece, jnp.float32),
+            pltpu.VMEM((2 * chunks,) + piece, jnp.float32),
+            pltpu.VMEM((chunks,) + piece, jnp.float32),
+            pltpu.VMEM((chunks,) + piece, jnp.float32),
+            pltpu.SemaphoreType.DMA((4, n_seq, pairs)),
+            pltpu.SemaphoreType.DMA((4, n_seq, pairs)),
+            pltpu.SemaphoreType.DMA((4, n_seq, pairs)),
+            pltpu.SemaphoreType.DMA((4,)),
             pltpu.SemaphoreType.DMA((3,)),
-            pltpu.SemaphoreType.DMA((3,)),
-            pltpu.SemaphoreType.DMA((3,)),
+            pltpu.SemaphoreType.DMA((3 * chunks,)),
+            pltpu.SemaphoreType.DMA((3 * chunks,)),
         ],
         compiler_params=pltpu.CompilerParams(collective_id=0, has_side_effects=True),
     )(queries, keys, values, out_grad, w_query, w_key, w_value)

time: 41.3 us -> 38.5 us (0.932)
  Pallas kernels: 39.5 us -> 36.8 us
    pallas_call x1, Pallas kernels: 39.5 us -> 36.8 us  [direct_form(): pl.pallas_call(functools.partial(direct_kernel, n_seq), out_shape=jax.Sha...]
where the time goes in v1:
time: 38.5 us; the launch traced here: 38.3 us
  Pallas kernels  36.8 us (96%)
  local copies, waits for them, and re-layouts  1.57 us (4%)
    pallas_call x1, Pallas kernels, direct_form(): pl.pallas_call(functools.partial(direct_kernel, n_seq), out_shape=jax.Sha...  36.8 us
    unnamed x1, local copies, waits for them, and re-layouts  1.57 us

profile of v1, /device:TPU:0, one launch (start us, length us, event | category | flops | bytes accessed | tf_op | source)
XLA Modules:
  0.0 38.3 jit_solution(8636628490010138570)
XLA Ops:
  0.0 36.8 %shard_map.73 = bf16[128,512]{1,0:T(8,128)(2,1)} custom-call(bf16[128,256]{1,0:T(8,128)(2,1)} %q_hbm.1, bf16[128,256]{1,0:T(8,128)(2,1)} %k_hbm.1, bf16[128,256]{1,0:T(8,128)(2,1)} %v_hbm.1, bf16[128,256]{1,0:T(8,128)(2,1)} %g_hbm.1, bf16[256,2048]{1,0:T(8,128)(2,1)} %wq_hbm.1, bf16[256,2048]{1,0:T(8,128)(2,1)} %wk_hbm.1, bf16[256,2048]{1,0:T(8,128)(2,1)} %wv_hbm.1), custom_call_target="tpu_custom_call" | custom-call | tf_op jit(solution)/shard_map/pallas_call | solution.py:517
  36.8 1.6 %copy.9 = bf16[128,512]{1,0:T(8,128)(2,1)} copy(bf16[128,512]{1,0:T(8,128)(2,1)} %shard_map.73) | data formatting | bytes 262144

commit v2 on v1

--- a/solution.py
+++ b/solution.py
@@ -203,29 +203,29 @@
     has_down = line > 0
     lower, upper = 2 * line < lines, 2 * line >= lines
 
+    barrier = pltpu.get_barrier_semaphore()
+
+    def greet(target):
+        pl.semaphore_signal(barrier, inc=1, device_id=target, device_id_type=MESH)
+
+    greet({"seq": other})
+    greet({"head": core_mate})
+    greet({"head": far_mate})
+
+    @pl.when(has_up)
+    def _():
+        greet({"seq": me + 2})
+
+    @pl.when(has_down)
+    def _():
+        greet({"seq": me - 2})
+
     own_copies = [
         pltpu.make_async_copy(source, own.at[i], own_sem.at[i])
         for i, source in enumerate((k_hbm, v_hbm, q_hbm, g_hbm))
     ]
     for copy in own_copies:
         copy.start()
-
-    barrier = pltpu.get_barrier_semaphore()
-
-    def greet(target):
-        pl.semaphore_signal(barrier, inc=1, device_id=target, device_id_type=MESH)
-
-    greet({"seq": other})
-    greet({"head": core_mate})
-    greet({"head": far_mate})
-
-    @pl.when(has_up)
-    def _():
-        greet({"seq": me + 2})
-
-    @pl.when(has_down)
-    def _():
-        greet({"seq": me - 2})
 
     weight_copies = [
         pltpu.make_async_copy(source, weights.at[i], weight_sem.at[i])

time: 38.5 us -> 38.5 us (level)
  no operation moved by 1% of the time
where the time goes in v2:
time: 38.5 us; the launch traced here: 38.4 us
  Pallas kernels  36.8 us (96%)
  local copies, waits for them, and re-layouts  1.57 us (4%)
    pallas_call x1, Pallas kernels, direct_form(): pl.pallas_call(functools.partial(direct_kernel, n_seq), out_shape=jax.Sha...  36.8 us
    unnamed x1, local copies, waits for them, and re-layouts  1.57 us

profile of v2, /device:TPU:0, one launch (start us, length us, event | category | flops | bytes accessed | tf_op | source)
XLA Modules:
  0.0 38.4 jit_solution(8332610440082703813)
XLA Ops:
  0.0 36.8 %shard_map.73 = bf16[128,512]{1,0:T(8,128)(2,1)} custom-call(bf16[128,256]{1,0:T(8,128)(2,1)} %q_hbm.1, bf16[128,256]{1,0:T(8,128)(2,1)} %k_hbm.1, bf16[128,256]{1,0:T(8,128)(2,1)} %v_hbm.1, bf16[128,256]{1,0:T(8,128)(2,1)} %g_hbm.1, bf16[256,2048]{1,0:T(8,128)(2,1)} %wq_hbm.1, bf16[256,2048]{1,0:T(8,128)(2,1)} %wk_hbm.1, bf16[256,2048]{1,0:T(8,128)(2,1)} %wv_hbm.1), custom_call_target="tpu_custom_call" | custom-call | tf_op jit(solution)/shard_map/pallas_call | solution.py:517
  36.8 1.6 %copy.9 = bf16[128,512]{1,0:T(8,128)(2,1)} copy(bf16[128,512]{1,0:T(8,128)(2,1)} %shard_map.73) | data formatting | bytes 262144
